TPU v7x, 512 devices: a whole 4x4x16 slice. The times are simulated.
512 devices in a mesh: section: 64 (over y, z_lo, core), coil: 8 (over z_hi, x).
Axes of the slice: x: 4, y: 4, z: 16 (z_hi: 2, z_lo: 8; z = z_hi * 8 + z_lo), core: 2. Of those that a mesh axis runs over, the one named last changes fastest.
Arguments:
- kspace: bfloat16 [16, 64, 64, 640], P('coil', None, 'section'), may hold values from -6 to 6
- coil_maps: bfloat16 [16, 64, 64, 640], P('coil', 'section'), may hold values from -1.5 to 1.5
- sampling: int32 [2, 32, 320], replicated, may hold values 0 or 1
- dc_weight: float32 [2], replicated, may hold values from 0.5 to 2.5
- kernel_in: float32 [2, 9, 18, 2], replicated, may hold values from -1.5 to 1.5
- bias_in: float32 [2, 18], replicated, may hold values from -0.5 to 0.5
- kernel_out: float32 [2, 9, 2, 18], replicated, may hold values from -0.5 to 0.5
- bias_out: float32 [2, 2], replicated, may hold values from -0.5 to 0.5
- cotangent: bfloat16 [64, 64, 640], P('section'), may hold values from -6 to 6
Outputs:
- image_out: float32 [64, 64, 640], P('section')
- grad_kspace: float32 [16, 64, 64, 640], P('coil', None, 'section')
All inputs are finite; a program needn't handle non-finite values.
Results may differ from a plain program's by a relative error of at most 0.035.
Values may be sent and summed in bfloat16 or wider, within the bound.
A program may use at most 64 MiB of HBM per device.

v0:
```python
import math
import jax
import jax.numpy as jnp
from jax import lax
from jax.sharding import PartitionSpec as P

CASCADES = 2
VOLUMES = 2
PRECISE = lax.Precision.HIGHEST


def line_table(count, exponent_sign):
    indices = jnp.arange(count, dtype=jnp.int32)
    product = indices[:, None] * indices[None, :] % count
    angles = product.astype(jnp.float32) * (2.0 * math.pi / count)
    factor = 1.0 / math.sqrt(count)
    return (jnp.cos(angles) * factor, exponent_sign * jnp.sin(angles) * factor)


def line_matrix(count, exponent_sign):
    real_part, imag_part = line_table(count, exponent_sign)
    upper_rows = jnp.concatenate([real_part, imag_part], axis=1)
    lower_rows = jnp.concatenate([-imag_part, real_part], axis=1)
    return jnp.concatenate([upper_rows, lower_rows], axis=0).astype(jnp.bfloat16)


def line_transform(values, matrix):
    return jnp.dot(values.astype(jnp.bfloat16), matrix, preferred_element_type=jnp.float32)


def depth_transform(values, volumes, exponent_sign):
    layout_shape = values.shape
    width_two = layout_shape[-1]
    half_width = width_two // 2
    depth_count = layout_shape[1] // volumes
    real_part, imag_part = line_table(depth_count, exponent_sign)
    blocks = values.astype(jnp.bfloat16).reshape(
        layout_shape[0], volumes, depth_count, layout_shape[2], width_two
    )
    straight = jnp.einsum(
        "kz,cvzrw->cvkrw",
        real_part.astype(jnp.bfloat16),
        blocks,
        preferred_element_type=jnp.float32,
    )
    crossed = jnp.einsum(
        "kz,cvzrw->cvkrw",
        imag_part.astype(jnp.bfloat16),
        blocks,
        preferred_element_type=jnp.float32,
    )
    turned = jnp.concatenate([-crossed[..., half_width:], crossed[..., :half_width]], axis=-1)
    return (straight + turned).reshape(layout_shape)


def spread(coil_maps, picture):
    half_width = coil_maps.shape[-1] // 2
    maps_real = coil_maps[..., :half_width].astype(jnp.float32)
    maps_imag = coil_maps[..., half_width:].astype(jnp.float32)
    pic_real = picture[..., :half_width].astype(jnp.float32)
    pic_imag = picture[..., half_width:].astype(jnp.float32)
    return jnp.concatenate(
        [maps_real * pic_real - maps_imag * pic_imag, maps_real * pic_imag + maps_imag * pic_real],
        axis=-1,
    )


def collect(coil_maps, coil_images):
    half_width = coil_maps.shape[-1] // 2
    maps_real = coil_maps[..., :half_width].astype(jnp.float32)
    maps_imag = coil_maps[..., half_width:].astype(jnp.float32)
    img_real = coil_images[..., :half_width]
    img_imag = coil_images[..., half_width:]
    summed = jnp.concatenate(
        [maps_real * img_real + maps_imag * img_imag, maps_real * img_imag - maps_imag * img_real],
        axis=-1,
    )
    return jnp.sum(summed, axis=0)


def shifted_windows(planes):
    row_count, col_count = (planes.shape[-2], planes.shape[-1])
    padded = jnp.pad(planes, ((0, 0), (1, 1), (1, 1)))
    return jnp.stack(
        [
            padded[:, row_shift : row_shift + row_count, col_shift : col_shift + col_count]
            for row_shift in range(3)
            for col_shift in range(3)
        ],
        axis=0,
    )


def conv_out(hidden, kernel, bias):
    row_count, col_count = (hidden.shape[-2], hidden.shape[-1])
    projected = jnp.einsum("toc,cxy->toxy", kernel, hidden, precision=PRECISE)
    padded = jnp.pad(projected, ((0, 0), (0, 0), (1, 1), (1, 1)))
    summed = jnp.zeros((kernel.shape[1], row_count, col_count), jnp.float32) + bias[:, None, None]
    for tap_index in range(9):
        row_shift = tap_index // 3
        col_shift = tap_index % 3
        summed = (
            summed
            + padded[
                tap_index, :, row_shift : row_shift + row_count, col_shift : col_shift + col_count
            ]
        )
    return summed


def refine(picture, kernel_in, bias_in, kernel_out, bias_out):
    half_width = picture.shape[-1] // 2
    planes = jnp.stack([picture[:, :half_width], picture[:, half_width:]], axis=0)
    hidden = (
        jnp.einsum("toc,tcxy->oxy", kernel_in, shifted_windows(planes), precision=PRECISE)
        + bias_in[:, None, None]
    )
    hidden = jax.nn.silu(hidden)
    output = conv_out(hidden, kernel_out, bias_out)
    return jnp.concatenate([output[0], output[1]], axis=1)


def body(
    kspace, coil_maps, sampling, dc_weight, kernel_in, bias_in, kernel_out, bias_out, cotangent
):
    width_two = kspace.shape[-1]
    slot_count = kspace.shape[1]
    lines_used = sampling.astype(jnp.float32).reshape(slot_count, width_two // 2)
    sampled = jnp.concatenate([lines_used, lines_used], axis=1)[None, :, None, :]
    measured = sampled * kspace.astype(jnp.float32)
    forward_line = line_matrix(width_two // 2, -1.0)
    inverse_line = line_matrix(width_two // 2, 1.0)

    def expand(picture):
        spreaded = spread(coil_maps, picture[None])
        line_out = line_transform(spreaded, forward_line).astype(jnp.bfloat16)
        moved = lax.all_to_all(line_out, "section", split_axis=2, concat_axis=1, tiled=True)
        return depth_transform(moved, VOLUMES, -1.0)

    def combine(kstate, is_final):
        depth_out = depth_transform(kstate, VOLUMES, 1.0).astype(jnp.bfloat16)
        moved = lax.all_to_all(depth_out, "section", split_axis=1, concat_axis=2, tiled=True)
        partial_sum = collect(coil_maps, line_transform(moved, inverse_line))
        summed = lax.psum(partial_sum.astype(jnp.bfloat16), "coil").astype(jnp.float32)
        if is_final:
            return summed
        return summed.astype(jnp.bfloat16)

    kstate = measured
    stored = []
    for cascade in range(CASCADES):
        picture = combine(kstate, False)[0].astype(jnp.float32)
        stored.append(picture)
        model = refine(
            picture, kernel_in[cascade], bias_in[cascade], kernel_out[cascade], bias_out[cascade]
        )
        update = expand(model.astype(jnp.bfloat16)[None])
        kstate = kstate - dc_weight[cascade] * sampled * (kstate - measured) + update
    image_out = combine(kstate, True)
    adjoint = expand(cotangent)
    grad_measured = jnp.zeros(measured.shape, jnp.float32)
    for cascade in reversed(range(CASCADES)):
        weighted = dc_weight[cascade] * sampled
        grad_measured = grad_measured + weighted * adjoint
        model_bar = combine(adjoint, False)[0].astype(jnp.float32)
        adjoint = adjoint - weighted * adjoint

        def local_model(flat, index=cascade):
            return refine(
                flat, kernel_in[index], bias_in[index], kernel_out[index], bias_out[index]
            )

        unused, pull_back = jax.vjp(local_model, stored[cascade])
        picture_bar = pull_back(model_bar)[0]
        adjoint = adjoint + expand(picture_bar.astype(jnp.bfloat16)[None])
    grad_measured = grad_measured + adjoint
    return (image_out, sampled * grad_measured)


def solution(mesh):
    return jax.shard_map(
        body,
        mesh=mesh,
        in_specs=(
            P("coil", None, "section", None),
            P("coil", "section", None, None),
            P(),
            P(),
            P(),
            P(),
            P(),
            P(),
            P("section", None, None),
        ),
        out_specs=(P("section", None, None), P("coil", None, "section", None)),
        check_vma=False,
    )
```

profile of v0, /device:TPU:1, one launch (start us, length us, event | category | flops | bytes accessed | tf_op | source)
XLA Modules:
  0.0 783.7 jit_solution(11465072695413646066)
XLA Ops:
  14.4 17.3 %all-to-all-start = ((bf16[2,64,1,640]{3,0,2,1:T(2,128)(2,1)}), bf16[2,64,1,640]{3,0,2,1:T(2,128)(2,1)S(1)}, u32[]{:S(2)}, u32[]{:S(2)}) async-start(bf16[2,64,1,640]{3,0,2,1:T(2,128)(2,1)} %copy.66), calls=%async_computation | async-start | bytes 327680 | tf_op jit(solution)/shard_map/all_to_all | solution.py:142
  36.8 10.5 %all-to-all-done = bf16[2,64,1,640]{3,0,2,1:T(2,128)(2,1)S(1)} async-done(((bf16[2,64,1,640]{3,0,2,1:T(2,128)(2,1)}), bf16[2,64,1,640]{3,0,2,1:T(2,128)(2,1)S(1)}, u32[]{:S(2)}, u32[]{:S(2)}) %all-to-all-start) | async-done | bytes 163872 | tf_op jit(solution)/shard_map/all_to_all | solution.py:142
  48.7 2.7 negate_convert_fusion
  51.4 131.9 %all-reduce.54.cloned.1.call-done = bf16[64,640]{1,0:T(8,128)(2,1)} async-done(((bf16[64,640]{1,0:T(8,128)(2,1)}), bf16[64,640]{1,0:T(8,128)(2,1)}) %all-reduce.54.cloned.1.call-update) | async-done | bytes 81936 | tf_op jit(solution)/shard_map/psum | solution.py:144
  194.6 6.9 stack.116
  205.3 3.3 fusion.34
  212.8 9.9 %all-to-all-start.5 = ((bf16[2,1,64,640]{3,0,1,2:T(2,128)(2,1)}), bf16[2,1,64,640]{3,0,1,2:T(2,128)(2,1)S(1)}, u32[]{:S(2)}, u32[]{:S(2)}) async-start(bf16[2,1,64,640]{3,0,1,2:T(2,128)(2,1)} %copy.103), calls=%async_computation.5 | async-start | bytes 327680 | tf_op jit(solution)/shard_map/all_to_all | solution.py:137
  224.0 14.3 %all-to-all-done.5 = bf16[2,1,64,640]{3,0,1,2:T(2,128)(2,1)S(1)} async-done(((bf16[2,1,64,640]{3,0,1,2:T(2,128)(2,1)}), bf16[2,1,64,640]{3,0,1,2:T(2,128)(2,1)S(1)}, u32[]{:S(2)}, u32[]{:S(2)}) %all-to-all-start.5) | async-done | bytes 163872 | tf_op jit(solution)/shard_map/all_to_all | solution.py:137
  238.2 6.8 all-to-all-start.1
  247.5 12.9 %all-to-all-done.1 = bf16[2,1,64,640]{3,0,1,2:T(2,128)(2,1)S(1)} async-done(((bf16[2,1,64,640]{3,0,1,2:T(2,128)(2,1)}), bf16[2,1,64,640]{3,0,1,2:T(2,128)(2,1)S(1)}, u32[]{:S(2)}, u32[]{:S(2)}) %all-to-all-start.1) | async-done | bytes 163872 | tf_op jit(solution)/shard_map/all_to_all | solution.py:137
  260.4 6.5 all-to-all-start.6
  270.5 12.0 %all-to-all-done.6 = bf16[2,64,1,640]{3,0,2,1:T(2,128)(2,1)S(1)} async-done(((bf16[2,64,1,640]{3,0,2,1:T(2,128)(2,1)}), bf16[2,64,1,640]{3,0,2,1:T(2,128)(2,1)S(1)}, u32[]{:S(2)}, u32[]{:S(2)}) %all-to-all-start.6) | async-done | bytes 163872 | tf_op jit(solution)/shard_map/all_to_all | solution.py:142
  282.4 6.5 all-to-all-start.2
  289.4 15.1 %all-to-all-done.2 = bf16[2,64,1,640]{3,0,2,1:T(2,128)(2,1)S(1)} async-done(((bf16[2,64,1,640]{3,0,2,1:T(2,128)(2,1)}), bf16[2,64,1,640]{3,0,2,1:T(2,128)(2,1)S(1)}, u32[]{:S(2)}, u32[]{:S(2)}) %all-to-all-start.2) | async-done | bytes 163872 | tf_op jit(solution)/shard_map/all_to_all | solution.py:142
  306.6 139.9 %all-reduce.58.cloned.1.call-done = (bf16[64,640]{1,0:T(8,128)(2,1)}, bf16[64,640]{1,0:T(8,128)(2,1)}) async-done(((bf16[64,640]{1,0:T(8,128)(2,1)}, bf16[64,640]{1,0:T(8,128)(2,1)}), (bf16[64,640]{1,0:T(8,128)(2,1)}, bf16[64,640]{1,0:T(8,128)(2,1)})) %all-reduce.58.cloned.1.call-update) | async-done | bytes 163856 | tf_op jit(solution)/shard_map/psum | solution.py:144
  460.9 7.1 stack.129
  470.4 3.3 fusion.37
  476.9 6.4 fusion.2
  483.3 4.1 fusion.31
  494.8 11.3 %all-to-all-start.7 = ((bf16[2,1,64,640]{3,0,1,2:T(2,128)(2,1)}), bf16[2,1,64,640]{3,0,1,2:T(2,128)(2,1)S(1)}, u32[]{:S(2)}, u32[]{:S(2)}) async-start(bf16[2,1,64,640]{3,0,1,2:T(2,128)(2,1)} %copy.119), calls=%async_computation.7 | async-start | bytes 327680 | tf_op jit(solution)/shard_map/all_to_all | solution.py:137
  508.1 13.5 %all-to-all-done.7 = bf16[2,1,64,640]{3,0,1,2:T(2,128)(2,1)S(1)} async-done(((bf16[2,1,64,640]{3,0,1,2:T(2,128)(2,1)}), bf16[2,1,64,640]{3,0,1,2:T(2,128)(2,1)S(1)}, u32[]{:S(2)}, u32[]{:S(2)}) %all-to-all-start.7) | async-done | bytes 163872 | tf_op jit(solution)/shard_map/all_to_all | solution.py:137
  521.6 6.5 all-to-all-start.3
  530.3 13.3 %all-to-all-done.3 = bf16[2,1,64,640]{3,0,1,2:T(2,128)(2,1)S(1)} async-done(((bf16[2,1,64,640]{3,0,1,2:T(2,128)(2,1)}), bf16[2,1,64,640]{3,0,1,2:T(2,128)(2,1)S(1)}, u32[]{:S(2)}, u32[]{:S(2)}) %all-to-all-start.3) | async-done | bytes 163872 | tf_op jit(solution)/shard_map/all_to_all | solution.py:137
  543.6 6.5 all-to-all-start.8
  552.9 12.7 %all-to-all-done.8 = bf16[2,64,1,640]{3,0,2,1:T(2,128)(2,1)S(1)} async-done(((bf16[2,64,1,640]{3,0,2,1:T(2,128)(2,1)}), bf16[2,64,1,640]{3,0,2,1:T(2,128)(2,1)S(1)}, u32[]{:S(2)}, u32[]{:S(2)}) %all-to-all-start.8) | async-done | bytes 163872 | tf_op jit(solution)/shard_map/all_to_all | solution.py:142
  565.6 6.5 all-to-all-start.4
  573.0 14.7 %all-to-all-done.4 = bf16[2,64,1,640]{3,0,2,1:T(2,128)(2,1)S(1)} async-done(((bf16[2,64,1,640]{3,0,2,1:T(2,128)(2,1)}), bf16[2,64,1,640]{3,0,2,1:T(2,128)(2,1)S(1)}, u32[]{:S(2)}, u32[]{:S(2)}) %all-to-all-start.4) | async-done | bytes 163872 | tf_op jit(solution)/shard_map/all_to_all | solution.py:142
  589.8 138.2 %all-reduce.56.cloned.1.call-done = (bf16[1,64,640]{2,1,0:T(8,128)(2,1)}, bf16[64,640]{1,0:T(8,128)(2,1)}) async-done(((bf16[1,64,640]{2,1,0:T(8,128)(2,1)}, bf16[64,640]{1,0:T(8,128)(2,1)}), (bf16[1,64,640]{2,1,0:T(8,128)(2,1)}, bf16[64,640]{1,0:T(8,128)(2,1)})) %all-reduce.56.cloned.1.call-update) | async-done | bytes 163856 | tf_op jit(solution)/shard_map/psum | solution.py:144
  731.8 6.2 fusion
  738.0 4.3 fusion.28
  747.9 11.3 %all-to-all-start.9 = ((bf16[2,1,64,640]{3,0,1,2:T(2,128)(2,1)}), bf16[2,1,64,640]{3,0,1,2:T(2,128)(2,1)S(1)}, u32[]{:S(2)}, u32[]{:S(2)}) async-start(bf16[2,1,64,640]{3,0,1,2:T(2,128)(2,1)} %copy.134), calls=%async_computation.9 | async-start | bytes 327680 | tf_op jit(solution)/shard_map/all_to_all | solution.py:137
  759.8 14.9 %all-to-all-done.9 = bf16[2,1,64,640]{3,0,1,2:T(2,128)(2,1)S(1)} async-done(((bf16[2,1,64,640]{3,0,1,2:T(2,128)(2,1)}), bf16[2,1,64,640]{3,0,1,2:T(2,128)(2,1)S(1)}, u32[]{:S(2)}, u32[]{:S(2)}) %all-to-all-start.9) | async-done | bytes 163872 | tf_op jit(solution)/shard_map/all_to_all | solution.py:137
  (260 shorter events, 91.3 us)
Async XLA Ops:
  11.6 24.4 %copy-start.33 = (f32[2,9,18,2]{2,3,1,0:T(2,128)S(1)}, f32[2,9,18,2]{2,3,1,0:T(2,128)}, u32[]{:S(2)}) copy-start(f32[2,9,18,2]{2,3,1,0:T(2,128)} %param.13) | copy-start | bytes 7780
  11.6 24.4 %copy-start.35 = (f32[2,18]{1,0:T(2,128)S(1)}, f32[2,18]{1,0:T(2,128)}, u32[]{:S(2)}) copy-start(f32[2,18]{1,0:T(2,128)} %param.14) | copy-start | bytes 436
  11.6 24.4 %copy-start.36 = (f32[2,2]{1,0:T(2,128)S(1)}, f32[2,2]{1,0:T(2,128)}, u32[]{:S(2)}) copy-start(f32[2,2]{1,0:T(2,128)} %param.16) | copy-start | bytes 52
  11.6 24.4 %copy-start.34 = (f32[2,9,2,18]{3,2,1,0:T(2,128)S(1)}, f32[2,9,2,18]{3,2,1,0:T(2,128)}, u32[]{:S(2)}) copy-start(f32[2,9,2,18]{3,2,1,0:T(2,128)} %param.15) | copy-start | bytes 7780
  11.7 24.4 %copy-start.31 = (bf16[1,64,640]{2,1,0:T(8,128)(2,1)S(1)}, bf16[1,64,640]{2,1,0:T(8,128)(2,1)}, u32[]{:S(2)}) copy-start(bf16[1,64,640]{2,1,0:T(8,128)(2,1)} %param.17) | copy-start | bytes 245764
  14.4 33.3 %copy-start = (bf16[2,1,64,640]{3,2,1,0:T(8,128)(2,1)S(1)}, bf16[2,1,64,640]{3,2,1,0:T(8,128)(2,1)}, u32[]{:S(2)}) copy-start(bf16[2,1,64,640]{3,2,1,0:T(8,128)(2,1)} %param.10) | copy-start | bytes 491524
  14.4 32.9 %all-to-all-start = ((bf16[2,64,1,640]{3,0,2,1:T(2,128)(2,1)}), bf16[2,64,1,640]{3,0,2,1:T(2,128)(2,1)S(1)}, u32[]{:S(2)}, u32[]{:S(2)}) async-start(bf16[2,64,1,640]{3,0,2,1:T(2,128)(2,1)} %copy.66), calls=%async_computation | async-start | bytes 327680 | tf_op jit(solution)/shard_map/all_to_all | solution.py:142
  31.8 151.5 %all-reduce.54.cloned.1.call-start = ((), (), s32[]{:S(2)}) async-start(), calls=%async_computation.10 | async-start | bytes 163840 | tf_op jit(solution)/shard_map/psum | solution.py:144
  34.0 13.9 %copy-start.18 = (bf16[320,320]{1,0:T(8,128)(2,1)}, bf16[320,320]{1,0:T(8,128)(2,1)S(1)}, u32[]{:S(2)}) copy-start(bf16[320,320]{1,0:T(8,128)(2,1)S(1)} %get-tuple-element.122) | copy-start | bytes 614404
  212.8 25.5 %all-to-all-start.5 = ((bf16[2,1,64,640]{3,0,1,2:T(2,128)(2,1)}), bf16[2,1,64,640]{3,0,1,2:T(2,128)(2,1)S(1)}, u32[]{:S(2)}, u32[]{:S(2)}) async-start(bf16[2,1,64,640]{3,0,1,2:T(2,128)(2,1)} %copy.103), calls=%async_computation.5 | async-start | bytes 327680 | tf_op jit(solution)/shard_map/all_to_all | solution.py:137
  238.2 22.2 %all-to-all-start.1 = ((bf16[2,1,64,640]{3,0,1,2:T(2,128)(2,1)}), bf16[2,1,64,640]{3,0,1,2:T(2,128)(2,1)S(1)}, u32[]{:S(2)}, u32[]{:S(2)}) async-start(bf16[2,1,64,640]{3,0,1,2:T(2,128)(2,1)} %copy.81), calls=%async_computation.1 | async-start | bytes 327680 | tf_op jit(solution)/shard_map/all_to_all | solution.py:137
  245.9 21.6 %copy-start.7 = (f32[64,640]{1,0:T(8,128)S(1)}, f32[64,640]{1,0:T(8,128)}, u32[]{:S(2)}) copy-start(f32[64,640]{1,0:T(8,128)} %get-tuple-element.99) | copy-start | bytes 491524
  245.9 21.6 %copy-start.9 = (bf16[2,64,1,640]{3,1,2,0:T(8,128)(2,1)S(1)}, bf16[2,64,1,640]{3,1,2,0:T(8,128)(2,1)}, u32[]{:S(2)}) copy-start(bf16[2,64,1,640]{3,1,2,0:T(8,128)(2,1)} %param.9) | copy-start | bytes 491524
  260.4 22.0 %all-to-all-start.6 = ((bf16[2,64,1,640]{3,0,2,1:T(2,128)(2,1)}), bf16[2,64,1,640]{3,0,2,1:T(2,128)(2,1)S(1)}, u32[]{:S(2)}, u32[]{:S(2)}) async-start(bf16[2,64,1,640]{3,0,2,1:T(2,128)(2,1)} %copy.107), calls=%async_computation.6 | async-start | bytes 327680 | tf_op jit(solution)/shard_map/all_to_all | solution.py:142
  267.6 21.4 %copy-start.26 = (bf16[320,320]{1,0:T(8,128)(2,1)S(1)}, bf16[320,320]{1,0:T(8,128)(2,1)}, u32[]{:S(2)}) copy-start(bf16[320,320]{1,0:T(8,128)(2,1)} %copy-done.25) | copy-start | bytes 614404
  267.6 21.4 %copy-start.29 = (bf16[320,320]{1,0:T(8,128)(2,1)S(1)}, bf16[320,320]{1,0:T(8,128)(2,1)}, u32[]{:S(2)}) copy-start(bf16[320,320]{1,0:T(8,128)(2,1)} %copy-done.28) | copy-start | bytes 614404
  282.4 22.0 %all-to-all-start.2 = ((bf16[2,64,1,640]{3,0,2,1:T(2,128)(2,1)}), bf16[2,64,1,640]{3,0,2,1:T(2,128)(2,1)S(1)}, u32[]{:S(2)}, u32[]{:S(2)}) async-start(bf16[2,64,1,640]{3,0,2,1:T(2,128)(2,1)} %copy.84), calls=%async_computation.2 | async-start | bytes 327680 | tf_op jit(solution)/shard_map/all_to_all | solution.py:142
  288.9 157.6 %all-reduce.58.cloned.1.call-start = ((), (), s32[]{:S(2)}) async-start(), calls=%async_computation.12 | async-start | bytes 327680 | tf_op jit(solution)/shard_map/psum | solution.py:144
  494.8 26.8 %all-to-all-start.7 = ((bf16[2,1,64,640]{3,0,1,2:T(2,128)(2,1)}), bf16[2,1,64,640]{3,0,1,2:T(2,128)(2,1)S(1)}, u32[]{:S(2)}, u32[]{:S(2)}) async-start(bf16[2,1,64,640]{3,0,1,2:T(2,128)(2,1)} %copy.119), calls=%async_computation.7 | async-start | bytes 327680 | tf_op jit(solution)/shard_map/all_to_all | solution.py:137
  507.3 21.4 %copy-start.2 = (f32[2,2,32,1,640]{4,2,1,0,3:T(8,128)S(1)}, f32[2,2,32,1,640]{4,2,1,0,3:T(8,128)}, u32[]{:S(2)}) copy-start(f32[2,2,32,1,640]{4,2,1,0,3:T(8,128)} %copy-done.1) | copy-start | bytes 983044
  521.6 22.0 %all-to-all-start.3 = ((bf16[2,1,64,640]{3,0,1,2:T(2,128)(2,1)}), bf16[2,1,64,640]{3,0,1,2:T(2,128)(2,1)S(1)}, u32[]{:S(2)}, u32[]{:S(2)}) async-start(bf16[2,1,64,640]{3,0,1,2:T(2,128)(2,1)} %copy.98), calls=%async_computation.3 | async-start | bytes 327680 | tf_op jit(solution)/shard_map/all_to_all | solution.py:137
  529.1 21.7 %copy-start.5 = (f32[64,640]{1,0:T(8,128)S(1)}, f32[64,640]{1,0:T(8,128)}, u32[]{:S(2)}) copy-start(f32[64,640]{1,0:T(8,128)} %get-tuple-element.98) | copy-start | bytes 491524
  529.1 21.7 %copy-start.10 = (bf16[2,64,1,640]{3,1,2,0:T(8,128)(2,1)S(1)}, bf16[2,64,1,640]{3,1,2,0:T(8,128)(2,1)}, u32[]{:S(2)}) copy-start(bf16[2,64,1,640]{3,1,2,0:T(8,128)(2,1)} %param.9) | copy-start | bytes 491524
  529.1 21.7 %copy-start.11 = (f32[2,64,1,640]{3,2,1,0:T(1,128)S(1)}, f32[2,64,1,640]{3,2,1,0:T(1,128)}, u32[]{:S(2)}) copy-start(f32[2,64,1,640]{3,2,1,0:T(1,128)} %get-tuple-element.7) | copy-start | bytes 983044
  543.6 22.0 %all-to-all-start.8 = ((bf16[2,64,1,640]{3,0,2,1:T(2,128)(2,1)}), bf16[2,64,1,640]{3,0,2,1:T(2,128)(2,1)S(1)}, u32[]{:S(2)}, u32[]{:S(2)}) async-start(bf16[2,64,1,640]{3,0,2,1:T(2,128)(2,1)} %copy.122), calls=%async_computation.8 | async-start | bytes 327680 | tf_op jit(solution)/shard_map/all_to_all | solution.py:142
  550.7 21.8 %copy-start.27 = (bf16[320,320]{1,0:T(8,128)(2,1)S(1)}, bf16[320,320]{1,0:T(8,128)(2,1)}, u32[]{:S(2)}) copy-start(bf16[320,320]{1,0:T(8,128)(2,1)} %copy-done.25) | copy-start | bytes 614404
  550.8 21.8 %copy-start.30 = (bf16[320,320]{1,0:T(8,128)(2,1)S(1)}, bf16[320,320]{1,0:T(8,128)(2,1)}, u32[]{:S(2)}) copy-start(bf16[320,320]{1,0:T(8,128)(2,1)} %copy-done.28) | copy-start | bytes 614404
  565.6 22.0 %all-to-all-start.4 = ((bf16[2,64,1,640]{3,0,2,1:T(2,128)(2,1)}), bf16[2,64,1,640]{3,0,2,1:T(2,128)(2,1)S(1)}, u32[]{:S(2)}, u32[]{:S(2)}) async-start(bf16[2,64,1,640]{3,0,2,1:T(2,128)(2,1)} %copy.101), calls=%async_computation.4 | async-start | bytes 327680 | tf_op jit(solution)/shard_map/all_to_all | solution.py:142
  572.1 155.9 %all-reduce.56.cloned.1.call-start = ((), (), s32[]{:S(2)}) async-start(), calls=%async_computation.11 | async-start | bytes 327680 | tf_op jit(solution)/shard_map/psum | solution.py:144
  747.0 28.4 %copy-start.6 = (f32[64,640]{1,0:T(8,128)S(1)}, f32[64,640]{1,0:T(8,128)}, u32[]{:S(2)}) copy-start(f32[64,640]{1,0:T(8,128)} %get-tuple-element.98) | copy-start | bytes 491524
  747.0 28.4 %copy-start.8 = (f32[64,640]{1,0:T(8,128)S(1)}, f32[64,640]{1,0:T(8,128)}, u32[]{:S(2)}) copy-start(f32[64,640]{1,0:T(8,128)} %get-tuple-element.99) | copy-start | bytes 491524
  747.9 26.8 %all-to-all-start.9 = ((bf16[2,1,64,640]{3,0,1,2:T(2,128)(2,1)}), bf16[2,1,64,640]{3,0,1,2:T(2,128)(2,1)S(1)}, u32[]{:S(2)}, u32[]{:S(2)}) async-start(bf16[2,1,64,640]{3,0,1,2:T(2,128)(2,1)} %copy.134), calls=%async_computation.9 | async-start | bytes 327680 | tf_op jit(solution)/shard_map/all_to_all | solution.py:137
  (18 other events, 80.4 us)
Sparse Core Ops, SparseCore 0:
  48.8 134.4 all-reduce.53
  306.7 139.7 all-reduce.57
  589.9 138.0 all-reduce.55
where the time goes:
time: 793 us; the launch traced here: 784 us
  waiting for transfers between devices  544 us (69%)
  starting transfers between devices  89.4 us (11%)
  local copies, waits for them, and re-layouts  56.6 us (7%)
  matrix products  41.5 us (5%)
  other arithmetic  36.8 us (5%)
  between operations  15.6 us (2%)
    psum x3, waiting for transfers between devices, combine(): lax.psum(partial_sum.astype(jnp.bfloat16), 'coil').astype(jnp.float32)  410 us
    all_to_all x5, waiting for transfers between devices, expand(): lax.all_to_all(line_out, 'section', split_axis=2, concat_axis=1, tiled=True)  68.9 us
    all_to_all x5, waiting for transfers between devices, combine(): lax.all_to_all(depth_out, 'section', split_axis=1, concat_axis=2, tiled=T...  64.9 us
    all_to_all x5, starting transfers between devices, expand(): lax.all_to_all(line_out, 'section', split_axis=2, concat_axis=1, tiled=True)  45.7 us
    all_to_all x5, starting transfers between devices, combine(): lax.all_to_all(depth_out, 'section', split_axis=1, concat_axis=2, tiled=T...  43.1 us
    another operation x22, local copies, waits for them, and re-layouts, shifted_windows(): jnp.stack([padded[:, row_shift:row_shift + row_count, col_shift:col_shift...  32 us
    dot_general x4, matrix products, conv_out(): projected = jnp.einsum('toc,cxy->toxy', kernel, hidden, precision=PRECISE)  19.1 us
  transfers between devices with their start and end apart: 13, of which 13 were waited for; matrix products, arithmetic and copies ran while one was open for 3% of the time, Pallas kernels for 0%

commit v1 on v0

--- a/solution.py
+++ b/solution.py
@@ -141,7 +141,9 @@
         depth_out = depth_transform(kstate, VOLUMES, 1.0).astype(jnp.bfloat16)
         moved = lax.all_to_all(depth_out, "section", split_axis=1, concat_axis=2, tiled=True)
         partial_sum = collect(coil_maps, line_transform(moved, inverse_line))
-        summed = lax.psum(partial_sum.astype(jnp.bfloat16), "coil").astype(jnp.float32)
+        summed = jnp.sum(lax.all_gather(partial_sum.astype(jnp.bfloat16), "coil"), axis=0).astype(
+            jnp.float32
+        )
         if is_final:
             return summed
         return summed.astype(jnp.bfloat16)

time: 793 us -> 687 us (0.87)
  the two profiles are of different devices: /device:TPU:1 before, /device:TPU:34 now
where the time goes in v1:
time: 687 us; the launch traced here: 678 us
  blocking collectives  358 us (52%)
  waiting for transfers between devices  108 us (16%)
  starting transfers between devices  83.2 us (12%)
  local copies, waits for them, and re-layouts  53.2 us (8%)
  matrix products  41.1 us (6%)
  other arithmetic  31.9 us (5%)
    all_gather x5, blocking collectives, combine(): lax.all_gather(partial_sum.astype(jnp.bfloat16), 'coil')  336 us
    all_to_all x5, waiting for transfers between devices, expand(): lax.all_to_all(line_out, 'section', split_axis=2, concat_axis=1, tiled=True)  66.2 us
    all_to_all x5, starting transfers between devices, expand(): lax.all_to_all(line_out, 'section', split_axis=2, concat_axis=1, tiled=True)  45.5 us
    all_to_all x4, waiting for transfers between devices, combine(): lax.all_to_all(depth_out, 'section', split_axis=1, concat_axis=2, tiled=T...  42.3 us
    all_to_all x4, starting transfers between devices, combine(): lax.all_to_all(depth_out, 'section', split_axis=1, concat_axis=2, tiled=T...  37.7 us
    another operation x22, local copies, waits for them, and re-layouts, shifted_windows(): jnp.stack([padded[:, row_shift:row_shift + row_count, col_shift:col_shift...  32.4 us
    all_to_all x1, blocking collectives, combine(): lax.all_to_all(depth_out, 'section', split_axis=1, concat_axis=2, tiled=T...  21.8 us
    dot_general x4, matrix products, conv_out(): projected = jnp.einsum('toc,cxy->toxy', kernel, hidden, precision=PRECISE)  18.9 us
  transfers between devices with their start and end apart: 9, of which 9 were waited for; matrix products, arithmetic and copies ran while one was open for 3% of the time, Pallas kernels for 0%

profile of v1, /device:TPU:34, one launch (start us, length us, event | category | flops | bytes accessed | tf_op | source)
XLA Modules:
  0.0 678.4 jit_solution(15907074989393326659)
XLA Ops:
  7.7 15.8 %all-to-all-start = ((bf16[2,64,1,640]{3,0,2,1:T(2,128)(2,1)}), bf16[2,64,1,640]{3,0,2,1:T(2,128)(2,1)S(1)}, u32[]{:S(2)}, u32[]{:S(2)}) async-start(bf16[2,64,1,640]{3,0,2,1:T(2,128)(2,1)} %copy.139), calls=%async_computation | async-start | bytes 327680 | tf_op jit(solution)/shard_map/all_to_all | solution.py:142
  31.2 7.0 %all-to-all-done = bf16[2,64,1,640]{3,0,2,1:T(2,128)(2,1)S(1)} async-done(((bf16[2,64,1,640]{3,0,2,1:T(2,128)(2,1)}), bf16[2,64,1,640]{3,0,2,1:T(2,128)(2,1)S(1)}, u32[]{:S(2)}, u32[]{:S(2)}) %all-to-all-start) | async-done | bytes 163872 | tf_op jit(solution)/shard_map/all_to_all | solution.py:142
  39.0 63.7 %all-gather = bf16[512,640]{1,0:T(8,128)(2,1)S(1)} all-gather(bf16[64,640]{1,0:T(8,128)(2,1)S(1)} %maximum_reduce_fusion), channel_id=2, replica_groups=mesh['section'=64,'coil'=8] {'coil'}, dimensions={0}, use_global_device_ids=true | all-gather | bytes 737280 | tf_op jit(solution)/shard_map/all_gather | solution.py:144
  112.5 6.9 %stack.116 = f32[9,2,64,320]{3,0,1,2:T(8,128)S(1)} concatenate(f32[1,2,64,320]{3,0,1,2:T(1,128)} %copy.143, f32[1,2,64,320]{3,0,1,2:T(1,128)} %copy.144, f32[1,2,64,320]{3,0,1,2:T(1,128)} %copy.145, f32[1,2,64,320]{3,0,1,2:T(1,128)} %copy.146, f32[1,2,64,320]{3,0,1,2:T(1,128)} %copy.147, f32[1,2,64,320]{3,0,1,2:T(1,128)} %copy.148, f32[1,2,64,320]{3,0,1,2:T(1,128)} %copy.149, ...), dimensions={0} | concatenate | bytes 2949120 | tf_op jit(solution)/shard_map/stack | solution.py:84
  123.2 3.3 fusion.34
  130.7 7.4 %all-to-all-start.1 = ((bf16[2,1,64,640]{3,0,1,2:T(2,128)(2,1)}), bf16[2,1,64,640]{3,0,1,2:T(2,128)(2,1)S(1)}, u32[]{:S(2)}, u32[]{:S(2)}) async-start(bf16[2,1,64,640]{3,0,1,2:T(2,128)(2,1)} %copy.154), calls=%async_computation.1 | async-start | bytes 327680 | tf_op jit(solution)/shard_map/all_to_all | solution.py:137
  139.3 13.4 %all-to-all-done.1 = bf16[2,1,64,640]{3,0,1,2:T(2,128)(2,1)S(1)} async-done(((bf16[2,1,64,640]{3,0,1,2:T(2,128)(2,1)}), bf16[2,1,64,640]{3,0,1,2:T(2,128)(2,1)S(1)}, u32[]{:S(2)}, u32[]{:S(2)}) %all-to-all-start.1) | async-done | bytes 163872 | tf_op jit(solution)/shard_map/all_to_all | solution.py:137
  152.7 7.3 %all-to-all-start.5 = ((bf16[2,1,64,640]{3,0,1,2:T(2,128)(2,1)}), bf16[2,1,64,640]{3,0,1,2:T(2,128)(2,1)S(1)}, u32[]{:S(2)}, u32[]{:S(2)}) async-start(bf16[2,1,64,640]{3,0,1,2:T(2,128)(2,1)} %copy.176), calls=%async_computation.5 | async-start | bytes 327680 | tf_op jit(solution)/shard_map/all_to_all | solution.py:137
  163.6 11.1 %all-to-all-done.5 = bf16[2,1,64,640]{3,0,1,2:T(2,128)(2,1)S(1)} async-done(((bf16[2,1,64,640]{3,0,1,2:T(2,128)(2,1)}), bf16[2,1,64,640]{3,0,1,2:T(2,128)(2,1)S(1)}, u32[]{:S(2)}, u32[]{:S(2)}) %all-to-all-start.5) | async-done | bytes 163872 | tf_op jit(solution)/shard_map/all_to_all | solution.py:137
  174.8 7.3 %all-to-all-start.2 = ((bf16[2,64,1,640]{3,0,2,1:T(2,128)(2,1)}), bf16[2,64,1,640]{3,0,2,1:T(2,128)(2,1)S(1)}, u32[]{:S(2)}, u32[]{:S(2)}) async-start(bf16[2,64,1,640]{3,0,2,1:T(2,128)(2,1)} %copy.157), calls=%async_computation.2 | async-start | bytes 327680 | tf_op jit(solution)/shard_map/all_to_all | solution.py:142
  184.6 12.2 %all-to-all-done.2 = bf16[2,64,1,640]{3,0,2,1:T(2,128)(2,1)S(1)} async-done(((bf16[2,64,1,640]{3,0,2,1:T(2,128)(2,1)}), bf16[2,64,1,640]{3,0,2,1:T(2,128)(2,1)S(1)}, u32[]{:S(2)}, u32[]{:S(2)}) %all-to-all-start.2) | async-done | bytes 163872 | tf_op jit(solution)/shard_map/all_to_all | solution.py:142
  196.8 7.3 %all-to-all-start.6 = ((bf16[2,64,1,640]{3,0,2,1:T(2,128)(2,1)}), bf16[2,64,1,640]{3,0,2,1:T(2,128)(2,1)S(1)}, u32[]{:S(2)}, u32[]{:S(2)}) async-start(bf16[2,64,1,640]{3,0,2,1:T(2,128)(2,1)} %copy.180), calls=%async_computation.6 | async-start | bytes 327680 | tf_op jit(solution)/shard_map/all_to_all | solution.py:142
  204.5 14.3 %all-to-all-done.6 = bf16[2,64,1,640]{3,0,2,1:T(2,128)(2,1)S(1)} async-done(((bf16[2,64,1,640]{3,0,2,1:T(2,128)(2,1)}), bf16[2,64,1,640]{3,0,2,1:T(2,128)(2,1)S(1)}, u32[]{:S(2)}, u32[]{:S(2)}) %all-to-all-start.6) | async-done | bytes 163872 | tf_op jit(solution)/shard_map/all_to_all | solution.py:142
  219.5 66.9 %all-gather.1 = bf16[512,640]{1,0:T(8,128)(2,1)S(1)} all-gather(bf16[64,640]{1,0:T(8,128)(2,1)S(1)} %maximum_reduce_fusion.1), channel_id=3, replica_groups=mesh['section'=64,'coil'=8] {'coil'}, dimensions={0}, use_global_device_ids=true | all-gather | bytes 737280 | tf_op jit(solution)/shard_map/all_gather | solution.py:144
  286.7 65.4 %all-gather.3 = bf16[512,640]{1,0:T(8,128)(2,1)S(1)} all-gather(bf16[64,640]{1,0:T(8,128)(2,1)S(1)} %maximum_reduce_fusion.3), channel_id=5, replica_groups=mesh['section'=64,'coil'=8] {'coil'}, dimensions={0}, use_global_device_ids=true | all-gather | bytes 737280 | tf_op jit(solution)/shard_map/all_gather | solution.py:144
  366.2 6.9 %stack.129 = f32[9,2,64,320]{3,0,1,2:T(8,128)S(1)} concatenate(f32[1,2,64,320]{3,0,1,2:T(1,128)} %copy.160, f32[1,2,64,320]{3,0,1,2:T(1,128)} %copy.161, f32[1,2,64,320]{3,0,1,2:T(1,128)} %copy.162, f32[1,2,64,320]{3,0,1,2:T(1,128)} %copy.163, f32[1,2,64,320]{3,0,1,2:T(1,128)} %copy.164, f32[1,2,64,320]{3,0,1,2:T(1,128)} %copy.165, f32[1,2,64,320]{3,0,1,2:T(1,128)} %copy.166, ...), dimensions={0} | concatenate | bytes 2949120 | tf_op jit(solution)/shard_map/stack | solution.py:84
  375.6 6.2 fusion.2
  381.8 4.1 fusion.31
  392.0 15.7 %all-to-all-start.7 = ((bf16[2,1,64,640]{3,0,1,2:T(2,128)(2,1)}), bf16[2,1,64,640]{3,0,1,2:T(2,128)(2,1)S(1)}, u32[]{:S(2)}, u32[]{:S(2)}) async-start(bf16[2,1,64,640]{3,0,1,2:T(2,128)(2,1)} %copy.192), calls=%async_computation.7 | async-start | bytes 327680 | tf_op jit(solution)/shard_map/all_to_all | solution.py:137
  408.5 14.0 %all-to-all-done.7 = bf16[2,1,64,640]{3,0,1,2:T(2,128)(2,1)S(1)} async-done(((bf16[2,1,64,640]{3,0,1,2:T(2,128)(2,1)}), bf16[2,1,64,640]{3,0,1,2:T(2,128)(2,1)S(1)}, u32[]{:S(2)}, u32[]{:S(2)}) %all-to-all-start.7) | async-done | bytes 163872 | tf_op jit(solution)/shard_map/all_to_all | solution.py:137
  424.6 7.3 %all-to-all-start.8 = ((bf16[2,64,1,640]{3,0,2,1:T(2,128)(2,1)}), bf16[2,64,1,640]{3,0,2,1:T(2,128)(2,1)S(1)}, u32[]{:S(2)}, u32[]{:S(2)}) async-start(bf16[2,64,1,640]{3,0,2,1:T(2,128)(2,1)} %copy.195), calls=%async_computation.8 | async-start | bytes 327680 | tf_op jit(solution)/shard_map/all_to_all | solution.py:142
  432.0 3.3 fusion.37
  437.8 8.8 %all-to-all-done.8 = bf16[2,64,1,640]{3,0,2,1:T(2,128)(2,1)S(1)} async-done(((bf16[2,64,1,640]{3,0,2,1:T(2,128)(2,1)}), bf16[2,64,1,640]{3,0,2,1:T(2,128)(2,1)S(1)}, u32[]{:S(2)}, u32[]{:S(2)}) %all-to-all-start.8) | async-done | bytes 163872 | tf_op jit(solution)/shard_map/all_to_all | solution.py:142
  447.4 67.3 %all-gather.4 = bf16[512,640]{1,0:T(8,128)(2,1)S(1)} all-gather(bf16[64,640]{1,0:T(8,128)(2,1)S(1)} %maximum_reduce_fusion.4), channel_id=6, replica_groups=mesh['section'=64,'coil'=8] {'coil'}, dimensions={0}, use_global_device_ids=true | all-gather | bytes 737280 | tf_op jit(solution)/shard_map/all_gather | solution.py:144
  516.9 6.2 fusion
  523.1 4.1 fusion.28
  533.1 7.8 %all-to-all-start.3 = ((bf16[2,1,64,640]{3,0,1,2:T(2,128)(2,1)}), bf16[2,1,64,640]{3,0,1,2:T(2,128)(2,1)S(1)}, u32[]{:S(2)}, u32[]{:S(2)}) async-start(bf16[2,1,64,640]{3,0,1,2:T(2,128)(2,1)} %copy.171), calls=%async_computation.3 | async-start | bytes 327680 | tf_op jit(solution)/shard_map/all_to_all | solution.py:137
  542.2 13.4 %all-to-all-done.3 = bf16[2,1,64,640]{3,0,1,2:T(2,128)(2,1)S(1)} async-done(((bf16[2,1,64,640]{3,0,1,2:T(2,128)(2,1)}), bf16[2,1,64,640]{3,0,1,2:T(2,128)(2,1)S(1)}, u32[]{:S(2)}, u32[]{:S(2)}) %all-to-all-start.3) | async-done | bytes 163872 | tf_op jit(solution)/shard_map/all_to_all | solution.py:137
  555.6 7.3 %all-to-all-start.9 = ((bf16[2,1,64,640]{3,0,1,2:T(2,128)(2,1)}), bf16[2,1,64,640]{3,0,1,2:T(2,128)(2,1)S(1)}, u32[]{:S(2)}, u32[]{:S(2)}) async-start(bf16[2,1,64,640]{3,0,1,2:T(2,128)(2,1)} %copy.207), calls=%async_computation.9 | async-start | bytes 327680 | tf_op jit(solution)/shard_map/all_to_all | solution.py:137
  563.4 14.2 %all-to-all-done.9 = bf16[2,1,64,640]{3,0,1,2:T(2,128)(2,1)S(1)} async-done(((bf16[2,1,64,640]{3,0,1,2:T(2,128)(2,1)}), bf16[2,1,64,640]{3,0,1,2:T(2,128)(2,1)S(1)}, u32[]{:S(2)}, u32[]{:S(2)}) %all-to-all-start.9) | async-done | bytes 163872 | tf_op jit(solution)/shard_map/all_to_all | solution.py:137
  582.1 21.8 %all_to_all.40 = bf16[2,64,1,640]{3,0,2,1:T(2,128)(2,1)S(1)} all-to-all(bf16[2,64,1,640]{3,0,2,1:T(2,128)(2,1)S(1)} %copy.174), channel_id=1, replica_groups=mesh['section'=64,'coil'=8] {'section'}, dimensions={1} | all-to-all | bytes 327680 | tf_op jit(solution)/shard_map/all_to_all | solution.py:142
  604.6 72.8 %all-gather.2 = bf16[512,640]{1,0:T(8,128)(2,1)S(1)} all-gather(bf16[64,640]{1,0:T(8,128)(2,1)S(1)} %maximum_reduce_fusion.2), channel_id=4, replica_groups=mesh['section'=64,'coil'=8] {'coil'}, dimensions={0}, use_global_device_ids=true | all-gather | bytes 737280 | tf_op jit(solution)/shard_map/all_gather | solution.py:144
  (268 shorter events, 85.3 us)
Async XLA Ops:
  5.0 25.4 %copy-start.37 = (f32[2,9,18,2]{2,3,1,0:T(2,128)S(1)}, f32[2,9,18,2]{2,3,1,0:T(2,128)}, u32[]{:S(2)}) copy-start(f32[2,9,18,2]{2,3,1,0:T(2,128)} %param.13) | copy-start | bytes 7780
  6.2 24.2 %copy-start.39 = (f32[2,18]{1,0:T(2,128)S(1)}, f32[2,18]{1,0:T(2,128)}, u32[]{:S(2)}) copy-start(f32[2,18]{1,0:T(2,128)} %param.14) | copy-start | bytes 436
  6.2 24.3 %copy-start.40 = (f32[2,2]{1,0:T(2,128)S(1)}, f32[2,2]{1,0:T(2,128)}, u32[]{:S(2)}) copy-start(f32[2,2]{1,0:T(2,128)} %param.16) | copy-start | bytes 52
  6.2 24.3 %copy-start.38 = (f32[2,9,2,18]{3,2,1,0:T(2,128)S(1)}, f32[2,9,2,18]{3,2,1,0:T(2,128)}, u32[]{:S(2)}) copy-start(f32[2,9,2,18]{3,2,1,0:T(2,128)} %param.15) | copy-start | bytes 7780
  6.2 24.3 %copy-start.36 = (bf16[1,64,640]{2,1,0:T(8,128)(2,1)S(1)}, bf16[1,64,640]{2,1,0:T(8,128)(2,1)}, u32[]{:S(2)}) copy-start(bf16[1,64,640]{2,1,0:T(8,128)(2,1)} %param.17) | copy-start | bytes 245764
  7.7 30.5 %all-to-all-start = ((bf16[2,64,1,640]{3,0,2,1:T(2,128)(2,1)}), bf16[2,64,1,640]{3,0,2,1:T(2,128)(2,1)S(1)}, u32[]{:S(2)}, u32[]{:S(2)}) async-start(bf16[2,64,1,640]{3,0,2,1:T(2,128)(2,1)} %copy.139), calls=%async_computation | async-start | bytes 327680 | tf_op jit(solution)/shard_map/all_to_all | solution.py:142
  23.6 15.1 %copy-start = (bf16[2,1,64,640]{3,2,1,0:T(8,128)(2,1)S(1)}, bf16[2,1,64,640]{3,2,1,0:T(8,128)(2,1)}, u32[]{:S(2)}) copy-start(bf16[2,1,64,640]{3,2,1,0:T(8,128)(2,1)} %param.10) | copy-start | bytes 491524
  25.8 13.1 %copy-start.20 = (bf16[320,320]{1,0:T(8,128)(2,1)}, bf16[320,320]{1,0:T(8,128)(2,1)S(1)}, u32[]{:S(2)}) copy-start(bf16[320,320]{1,0:T(8,128)(2,1)S(1)} %get-tuple-element.117) | copy-start | bytes 614404
  25.8 13.1 %copy-start.23 = (bf16[320,320]{1,0:T(8,128)(2,1)}, bf16[320,320]{1,0:T(8,128)(2,1)S(1)}, u32[]{:S(2)}) copy-start(bf16[320,320]{1,0:T(8,128)(2,1)S(1)} %get-tuple-element.118) | copy-start | bytes 614404
  27.7 11.1 %copy-start.27 = (bf16[320,320]{1,0:T(8,128)(2,1)}, bf16[320,320]{1,0:T(8,128)(2,1)S(1)}, u32[]{:S(2)}) copy-start(bf16[320,320]{1,0:T(8,128)(2,1)S(1)} %fusion.80) | copy-start | bytes 614404
  130.7 22.1 %all-to-all-start.1 = ((bf16[2,1,64,640]{3,0,1,2:T(2,128)(2,1)}), bf16[2,1,64,640]{3,0,1,2:T(2,128)(2,1)S(1)}, u32[]{:S(2)}, u32[]{:S(2)}) async-start(bf16[2,1,64,640]{3,0,1,2:T(2,128)(2,1)} %copy.154), calls=%async_computation.1 | async-start | bytes 327680 | tf_op jit(solution)/shard_map/all_to_all | solution.py:137
  138.5 22.2 %copy-start.8 = (bf16[2,64,1,640]{3,1,2,0:T(8,128)(2,1)S(1)}, bf16[2,64,1,640]{3,1,2,0:T(8,128)(2,1)}, u32[]{:S(2)}) copy-start(bf16[2,64,1,640]{3,1,2,0:T(8,128)(2,1)} %param.9) | copy-start | bytes 491524
  138.5 22.2 %copy-start.10 = (f32[64,640]{1,0:T(8,128)S(1)}, f32[64,640]{1,0:T(8,128)}, u32[]{:S(2)}) copy-start(f32[64,640]{1,0:T(8,128)} %get-tuple-element.95) | copy-start | bytes 491524
  152.7 22.0 %all-to-all-start.5 = ((bf16[2,1,64,640]{3,0,1,2:T(2,128)(2,1)}), bf16[2,1,64,640]{3,0,1,2:T(2,128)(2,1)S(1)}, u32[]{:S(2)}, u32[]{:S(2)}) async-start(bf16[2,1,64,640]{3,0,1,2:T(2,128)(2,1)} %copy.176), calls=%async_computation.5 | async-start | bytes 327680 | tf_op jit(solution)/shard_map/all_to_all | solution.py:137
  174.8 22.0 %all-to-all-start.2 = ((bf16[2,64,1,640]{3,0,2,1:T(2,128)(2,1)}), bf16[2,64,1,640]{3,0,2,1:T(2,128)(2,1)S(1)}, u32[]{:S(2)}, u32[]{:S(2)}) async-start(bf16[2,64,1,640]{3,0,2,1:T(2,128)(2,1)} %copy.157), calls=%async_computation.2 | async-start | bytes 327680 | tf_op jit(solution)/shard_map/all_to_all | solution.py:142
  182.3 21.7 %copy-start.21 = (bf16[320,320]{1,0:T(8,128)(2,1)S(1)}, bf16[320,320]{1,0:T(8,128)(2,1)}, u32[]{:S(2)}) copy-start(bf16[320,320]{1,0:T(8,128)(2,1)} %copy-done.20) | copy-start | bytes 614404
  182.3 21.7 %copy-start.28 = (bf16[320,320]{1,0:T(8,128)(2,1)S(1)}, bf16[320,320]{1,0:T(8,128)(2,1)}, u32[]{:S(2)}) copy-start(bf16[320,320]{1,0:T(8,128)(2,1)} %copy-done.27) | copy-start | bytes 614404
  196.8 22.0 %all-to-all-start.6 = ((bf16[2,64,1,640]{3,0,2,1:T(2,128)(2,1)}), bf16[2,64,1,640]{3,0,2,1:T(2,128)(2,1)S(1)}, u32[]{:S(2)}, u32[]{:S(2)}) async-start(bf16[2,64,1,640]{3,0,2,1:T(2,128)(2,1)} %copy.180), calls=%async_computation.6 | async-start | bytes 327680 | tf_op jit(solution)/shard_map/all_to_all | solution.py:142
  390.4 17.3 %copy-start.14 = (f32[2,32,320]{2,1,0:T(8,128)S(1)}, f32[2,32,320]{2,1,0:T(8,128)}, u32[]{:S(2)}) copy-start(f32[2,32,320]{2,1,0:T(8,128)} %copy-done.13) | copy-start | bytes 245764
  391.1 32.0 %copy-start.2 = (f32[2,2,32,1,640]{4,2,1,0,3:T(8,128)S(1)}, f32[2,2,32,1,640]{4,2,1,0,3:T(8,128)}, u32[]{:S(2)}) copy-start(f32[2,2,32,1,640]{4,2,1,0,3:T(8,128)} %copy-done.1) | copy-start | bytes 983044
  392.0 30.4 %all-to-all-start.7 = ((bf16[2,1,64,640]{3,0,1,2:T(2,128)(2,1)}), bf16[2,1,64,640]{3,0,1,2:T(2,128)(2,1)S(1)}, u32[]{:S(2)}, u32[]{:S(2)}) async-start(bf16[2,1,64,640]{3,0,1,2:T(2,128)(2,1)} %copy.192), calls=%async_computation.7 | async-start | bytes 327680 | tf_op jit(solution)/shard_map/all_to_all | solution.py:137
  422.8 9.1 %copy-start.7 = (f32[64,320,18,1]{1,2,3,0:T(8,128)S(1)}, f32[64,320,18,1]{1,2,3,0:T(8,128)}, u32[]{:S(2)}) copy-start(f32[64,320,18,1]{1,2,3,0:T(8,128)} %copy-done.6) | copy-start | bytes 4423684
  424.6 22.0 %all-to-all-start.8 = ((bf16[2,64,1,640]{3,0,2,1:T(2,128)(2,1)}), bf16[2,64,1,640]{3,0,2,1:T(2,128)(2,1)S(1)}, u32[]{:S(2)}, u32[]{:S(2)}) async-start(bf16[2,64,1,640]{3,0,2,1:T(2,128)(2,1)} %copy.195), calls=%async_computation.8 | async-start | bytes 327680 | tf_op jit(solution)/shard_map/all_to_all | solution.py:142
  436.2 10.5 %copy-start.22 = (bf16[320,320]{1,0:T(8,128)(2,1)S(1)}, bf16[320,320]{1,0:T(8,128)(2,1)}, u32[]{:S(2)}) copy-start(bf16[320,320]{1,0:T(8,128)(2,1)} %copy-done.20) | copy-start | bytes 614404
  436.2 10.5 %copy-start.26 = (bf16[320,320]{1,0:T(8,128)(2,1)S(1)}, bf16[320,320]{1,0:T(8,128)(2,1)}, u32[]{:S(2)}) copy-start(bf16[320,320]{1,0:T(8,128)(2,1)} %copy-done.23) | copy-start | bytes 614404
  436.2 10.5 %copy-start.29 = (bf16[320,320]{1,0:T(8,128)(2,1)S(1)}, bf16[320,320]{1,0:T(8,128)(2,1)}, u32[]{:S(2)}) copy-start(bf16[320,320]{1,0:T(8,128)(2,1)} %copy-done.27) | copy-start | bytes 614404
  533.1 22.5 %all-to-all-start.3 = ((bf16[2,1,64,640]{3,0,1,2:T(2,128)(2,1)}), bf16[2,1,64,640]{3,0,1,2:T(2,128)(2,1)S(1)}, u32[]{:S(2)}, u32[]{:S(2)}) async-start(bf16[2,1,64,640]{3,0,1,2:T(2,128)(2,1)} %copy.171), calls=%async_computation.3 | async-start | bytes 327680 | tf_op jit(solution)/shard_map/all_to_all | solution.py:137
  555.6 22.0 %all-to-all-start.9 = ((bf16[2,1,64,640]{3,0,1,2:T(2,128)(2,1)}), bf16[2,1,64,640]{3,0,1,2:T(2,128)(2,1)S(1)}, u32[]{:S(2)}, u32[]{:S(2)}) async-start(bf16[2,1,64,640]{3,0,1,2:T(2,128)(2,1)} %copy.207), calls=%async_computation.9 | async-start | bytes 327680 | tf_op jit(solution)/shard_map/all_to_all | solution.py:137
  563.0 15.6 %copy-start.9 = (bf16[2,64,1,640]{3,1,2,0:T(8,128)(2,1)S(1)}, bf16[2,64,1,640]{3,1,2,0:T(8,128)(2,1)}, u32[]{:S(2)}) copy-start(bf16[2,64,1,640]{3,1,2,0:T(8,128)(2,1)} %param.9) | copy-start | bytes 491524
  563.0 15.6 %copy-start.11 = (f32[64,640]{1,0:T(8,128)S(1)}, f32[64,640]{1,0:T(8,128)}, u32[]{:S(2)}) copy-start(f32[64,640]{1,0:T(8,128)} %get-tuple-element.95) | copy-start | bytes 491524
  563.0 15.6 %copy-start.12 = (f32[2,64,1,640]{3,2,1,0:T(1,128)S(1)}, f32[2,64,1,640]{3,2,1,0:T(1,128)}, u32[]{:S(2)}) copy-start(f32[2,64,1,640]{3,2,1,0:T(1,128)} %get-tuple-element.3) | copy-start | bytes 983044
  563.0 15.6 %copy-start.17 = (f32[64,640]{1,0:T(8,128)S(1)}, f32[64,640]{1,0:T(8,128)}, u32[]{:S(2)}) copy-start(f32[64,640]{1,0:T(8,128)} %get-tuple-element.94) | copy-start | bytes 491524
  (18 other events, 43.4 us)
